TPU v7x, 128 devices: a whole 4x4x4 slice. The times are simulated.
128 devices in a mesh: dp: 8 (over y, z_hi), proto: 16 (over z_lo, x, core).
Axes of the slice: x: 4, y: 4, z: 4 (z_hi: 2, z_lo: 2; z = z_hi * 2 + z_lo), core: 2. Of those that a mesh axis runs over, the one named last changes fastest.
Arguments:
- student_patch: bfloat16 [8, 2048, 256], P('dp', 'proto'), may hold values from -4 to 4
- teacher_patch: bfloat16 [8, 2048, 256], P('dp', 'proto'), may hold values from -4 to 4
- patch_image: int32 [8, 2048], P('dp', 'proto'), may hold values from 0 to 7, never falling along the last dimension, each value on 1 to 512 neighbouring positions
- masked_rows: int32 [8, 1024], P('dp', 'proto'), may hold values from 0 to 127, as said below
- student_proto: float32 [256, 131072], P(None, 'proto'), as said below
- teacher_proto: float32 [256, 131072], P(None, 'proto'), as said below
- first_moment: float32 [256, 131072], P('dp', 'proto'), as said below
- second_moment: float32 [256, 131072], P('dp', 'proto'), as said below
- centre: float32 [131072], P('proto'), may hold values from -0.3 to 0.3
Outputs:
- row_grad: float32 [8, 1024, 256], P('dp', 'proto')
- new_student: float32 [256, 131072], P('dp', 'proto')
- new_first: float32 [256, 131072], P('dp', 'proto')
- new_second: float32 [256, 131072], P('dp', 'proto')
- new_teacher: float32 [256, 131072], P('dp', 'proto')
- loss: float32 [], replicated
Inputs may be any that keep to these rules, and one draw needn't show every extreme that they name: `masked_rows`: for each data group and each index of proto in order, 64 distinct positions among that device's 128 patches, ascending; position 0 and position 127 of every device are always masked. `student_proto`: finite entries. `teacher_proto`: finite entries. `first_moment`: finite entries. `second_moment`: positive entries.
All inputs are finite; a program needn't handle non-finite values.
Results may differ from a plain program's by a relative error of at most 0.014.
Values may be sent and summed in bfloat16 or wider, within the bound.
A program may use at most 256 MiB of HBM per device.

v0:
```python
import jax
import jax.numpy as jnp
from jax import lax
from jax.sharding import PartitionSpec as P

PATCH_IMG = 256
student_temp = 0.1
teacher_temp = 0.07
beta_one = 0.9
beta_two = 0.999
fix_one = 0.9999734386011124
fix_two = 0.09520785288629038
learn_rate = 0.002
decay_rate = 0.04
teacher_keep = 0.994


def unit_rows(raw_rows):
    inverse = lax.rsqrt(jnp.sum(raw_rows * raw_rows, axis=-1, keepdims=True) + 1e-06)
    return (raw_rows * inverse, inverse)


def local(
    student_patch,
    teacher_patch,
    patch_image,
    masked_rows,
    student_proto,
    teacher_proto,
    first_moment,
    second_moment,
    centre,
):
    picked = masked_rows[0]
    mask_count = picked.shape[0]
    patch_count = patch_image.shape[1]
    proto_count = lax.axis_size("proto")
    data_count = lax.axis_size("dp")
    raw_student = student_patch[0][picked].astype(jnp.float32)
    raw_teacher = teacher_patch[0][picked].astype(jnp.float32)
    unit_student, inv_student = unit_rows(raw_student)
    unit_teacher, inv_teacher = unit_rows(raw_teacher)
    stacked = jnp.stack([unit_student, unit_teacher]).astype(jnp.bfloat16)
    gathered, image_ids = (
        lax.all_gather(stacked, "proto", axis=1, tiled=True),
        lax.all_gather(patch_image[0][picked], "proto", axis=0, tiled=True),
    )
    rows_student = gathered[0]
    rows_teacher = gathered[1]
    student_w = student_proto.astype(jnp.bfloat16)
    teacher_w = teacher_proto.astype(jnp.bfloat16)
    student_logit = (
        jnp.dot(rows_student, student_w, preferred_element_type=jnp.float32) / student_temp
    )
    teacher_raw = jnp.dot(rows_teacher, teacher_w, preferred_element_type=jnp.float32)
    teacher_logit = (teacher_raw - centre) / teacher_temp
    peak_s, peak_t = lax.pmax(
        (jnp.max(student_logit, axis=1), jnp.max(teacher_logit, axis=1)), "proto"
    )
    exp_s = jnp.exp(student_logit - peak_s[:, None])
    exp_t = jnp.exp(teacher_logit - peak_t[:, None])
    total_s, total_t = lax.psum((jnp.sum(exp_s, axis=1), jnp.sum(exp_t, axis=1)), "proto")
    prob_s = exp_s / total_s[:, None]
    prob_t = exp_t / total_t[:, None]
    labels = jnp.arange(patch_count * proto_count // PATCH_IMG, dtype=jnp.int32)
    matches = (image_ids[:, None] == labels[None, :]).astype(jnp.float32)
    counts = jnp.sum(matches, axis=0)
    per_row = jnp.dot(matches, counts, precision=lax.Precision.HIGHEST)
    row_ratio = mask_count * PATCH_IMG / patch_count
    weights = row_ratio / per_row
    log_total = peak_s + jnp.log(total_s)
    partial_loss = jnp.sum(weights * jnp.sum(prob_t * (log_total[:, None] - student_logit), axis=1))
    grad_logit = (weights[:, None] * (prob_s - prob_t) / student_temp).astype(jnp.bfloat16)
    unit_grad = lax.psum_scatter(
        lax.dot_general(
            grad_logit, student_w, (((1,), (1,)), ((), ())), preferred_element_type=jnp.float32
        ).astype(jnp.bfloat16),
        "proto",
        scatter_dimension=0,
        tiled=True,
    ).astype(jnp.float32)
    row_grad = (
        inv_student * unit_grad
        - inv_student
        * inv_student
        * inv_student
        * raw_student
        * jnp.sum(raw_student * unit_grad, axis=-1, keepdims=True)
    )
    slab_rows = first_moment.shape[0]
    slab_start = lax.axis_index("dp") * slab_rows
    proto_grad = lax.psum_scatter(
        lax.dot_general(
            rows_student, grad_logit, (((0,), (0,)), ((), ())), preferred_element_type=jnp.float32
        ).astype(jnp.bfloat16),
        "dp",
        scatter_dimension=0,
        tiled=True,
    ).astype(jnp.float32)
    loss_sum = lax.psum(partial_loss, ("dp", "proto"))
    rows_total = mask_count * proto_count * data_count
    own_student = lax.dynamic_slice_in_dim(student_proto, slab_start, slab_rows, 0)
    own_teacher = lax.dynamic_slice_in_dim(teacher_proto, slab_start, slab_rows, 0)
    new_first = beta_one * first_moment + (1.0 - beta_one) * proto_grad
    new_second = beta_two * second_moment + (1.0 - beta_two) * proto_grad * proto_grad
    step_size = new_first / fix_one / (jnp.sqrt(new_second / fix_two) + 1e-08)
    new_student = own_student - learn_rate * (step_size + decay_rate * own_student)
    new_teacher = teacher_keep * own_teacher + (1.0 - teacher_keep) * new_student
    loss = loss_sum / rows_total
    return (row_grad[None], new_student, new_first, new_second, new_teacher, loss)


def solution(mesh):
    in_specs = (
        P("dp", "proto", None),
        P("dp", "proto", None),
        P("dp", "proto"),
        P("dp", "proto"),
        P(None, "proto"),
        P(None, "proto"),
        P("dp", "proto"),
        P("dp", "proto"),
        P("proto"),
    )
    out_specs = (
        P("dp", "proto", None),
        P("dp", "proto"),
        P("dp", "proto"),
        P("dp", "proto"),
        P("dp", "proto"),
        P(),
    )
    return jax.shard_map(local, mesh=mesh, in_specs=in_specs, out_specs=out_specs, check_vma=False)
```

profile of v0, /device:TPU:0, one launch (start us, length us, event | category | flops | bytes accessed | tf_op | source)
XLA Modules:
  0.0 364.9 jit_solution(13910082086111725495)
XLA Ops:
  7.2 0.7 fusion.27
  7.9 0.1 copy-done
  8.0 0.7 gather_fusion
  8.7 0.1 fusion.20
  8.8 1.5 gather_fusion.2
  10.3 0.1 fusion.19
  10.5 0.1 fusion.18
  10.6 0.6 pad_maximum_fusion
  11.3 1.4 gather_fusion.1
  12.7 1.2 dynamic-slice
  14.6 0.2 dynamic-update-slice
  14.9 12.9 %all-reduce = s32[1024]{0:T(1024)S(1)} all-reduce(s32[1024]{0:T(1024)S(1)} %dynamic-update-slice), channel_id=2, replica_groups=mesh['dp'=8,'proto'=16] {'proto'}, use_global_device_ids=true, to_apply=%add | all-reduce | flops 1024 | bytes 8192
  27.8 0.1 convert_reduce_fusion
  27.9 0.1 fusion.25
  28.0 18.0 %all-gather.3.cloned.1.call-done = bf16[2,1024,256]{2,1,0:T(8,128)(2,1)} async-done(((bf16[2,64,256]{2,1,0:T(8,128)(2,1)}), bf16[2,1024,256]{2,1,0:T(8,128)(2,1)}) %all-gather.3.cloned.1.call-update) | async-done | bytes 1048592 | tf_op jit(solution)/shard_map/all_gather | solution.py:45
  46.1 16.0 %multiply_reduce_fusion.1 = (f32[1024]{0:T(1024)S(1)}, f32[1024,8192]{1,0:T(8,128)}) fusion(f32[256,8192]{1,0:T(8,128)} %param.13, bf16[2,1024,256]{2,1,0:T(8,128)(2,1)} %all-gather.3.cloned.1.call-done), kind=kOutput, calls=%fused_computation.10 | convolution fusion | flops 4313840640 | bytes 42471424 | tf_op jit(solution)/shard_map/dot_general | solution.py:53
  62.0 13.4 %fusion.1 = (f32[1024]{0:T(1024)S(1)}, f32[1024,8192]{1,0:T(8,128)}) fusion(f32[8192]{0:T(1024)S(1)} %copy-done.6, f32[256,8192]{1,0:T(8,128)S(1)} %copy-done.3, bf16[2,1024,256]{2,1,0:T(8,128)(2,1)S(1)} %copy-done.4), kind=kOutput, calls=%fused_computation.9 | convolution fusion | flops 4322229248 | bytes 42504192 | tf_op jit(solution)/shard_map/dot_general | solution.py:55
  75.5 29.6 %all-reduce.2 = (f32[1024]{0:T(1024)S(1)}, f32[1024]{0:T(1024)S(1)}) all-reduce(f32[1024]{0:T(1024)S(1)} %get-tuple-element.18, f32[1024]{0:T(1024)S(1)} %get-tuple-element.20), channel_id=1, replica_groups=mesh['dp'=8,'proto'=16] {'proto'}, use_global_device_ids=true, to_apply=%region_4.0 | all-reduce | flops 2048 | bytes 16384 | tf_op jit(solution)/shard_map/pmax | solution.py:57
  105.1 15.3 %fusion.3 = f32[1024]{0:T(1024)S(1)} fusion(f32[1024,8192]{1,0:T(8,128)} %get-tuple-element.21, f32[1024]{0:T(1024)S(1)} %get-tuple-element.9, f32[8192]{0:T(1024)S(1)} %copy-done.6), kind=kLoop, calls=%fused_computation.12 | loop fusion | flops 33553408 | bytes 33595392 | tf_op jit(solution)/shard_map/reduce_sum | solution.py:62
  120.4 4.8 %copy-done.2 = f32[1024,8192]{1,0:T(8,128)S(1)} copy-done((f32[1024,8192]{1,0:T(8,128)S(1)}, f32[1024,8192]{1,0:T(8,128)}, u32[]{:S(2)}) %copy-start.2) | copy-done | bytes 33554456
  125.2 6.7 %fusion = f32[1024]{0:T(1024)S(1)} fusion(f32[1024,8192]{1,0:T(8,128)S(1)} %copy-done.2, f32[1024]{0:T(1024)S(1)} %get-tuple-element.8), kind=kLoop, calls=%fused_computation.8 | loop fusion | flops 25164800 | bytes 33562624 | tf_op jit(solution)/shard_map/reduce_sum | solution.py:62
  131.9 27.8 %all-reduce.1 = (f32[1024]{0:T(1024)S(1)}, f32[1024]{0:T(1024)S(1)}) all-reduce(f32[1024]{0:T(1024)S(1)} %fusion, f32[1024]{0:T(1024)S(1)} %fusion.3), channel_id=1, replica_groups=mesh['dp'=8,'proto'=16] {'proto'}, use_global_device_ids=true, to_apply=%region_6.0 | all-reduce | flops 2048 | bytes 16384 | tf_op jit(solution)/shard_map/psum | solution.py:62
  159.7 31.3 %multiply_reduce_fusion = (f32[1024]{0:T(1024)S(1)}, bf16[1024,8192]{1,0:T(8,128)(2,1)}) fusion(f32[1024,8192]{1,0:T(8,128)} %get-tuple-element.19, f32[1024]{0:T(1024)S(1)} %log_add_fusion, f32[1024]{0:T(1024)S(1)} %get-tuple-element.7, f32[1024]{0:T(1024)S(1)} %get-tuple-element.9, f32[1024,8192]{1,0:T(8,128)} %get-tuple-element.21, f32[8192]{0:T(1024)S(1)} %copy-done.6, ...), kind=kLoop, calls=%fused_computation.3 | loop fusion | flops 117439488 | bytes 83947520 | tf_op jit(solution)/shard_map/reduce_sum | solution.py:72
  191.0 13.6 %fusion.10 = bf16[1024,256]{1,0:T(8,128)(2,1)} fusion(bf16[1024,8192]{1,0:T(8,128)(2,1)} %get-tuple-element.15, f32[256,8192]{1,0:T(8,128)} %param.13), kind=kOutput, calls=%fused_computation.22 | convolution fusion | flops 4297326592 | bytes 25690112 | tf_op jit(solution)/shard_map/dot_general | solution.py:75
  204.6 0.0 reduce-scatter.5.cloned.1.call-start
  204.7 12.1 %convolution_convert_fusion = bf16[256,8192]{1,0:T(8,128)(2,1)} fusion(bf16[1024,8192]{1,0:T(8,128)(2,1)} %get-tuple-element.15, bf16[2,1024,256]{2,1,0:T(8,128)(2,1)S(1)} %copy-done.4), kind=kOutput, calls=%fused_computation.13 | convolution fusion | flops 4297064448 | bytes 21495808 | tf_op jit(solution)/shard_map/dot_general | solution.py:93
  216.7 0.6 multiply_reduce_fusion.2
  217.4 66.2 %psum.23 = f32[]{:T(128)} all-reduce(f32[]{:T(128)} %multiply_reduce_fusion.2), channel_id=1, replica_groups=mesh['dp'=8,'proto'=16] {'dp','proto'}, use_global_device_ids=true, to_apply=%region_16.0 | all-reduce | flops 1 | bytes 8 | tf_op jit(solution)/shard_map/psum | solution.py:100
  284.3 0.9 fusion.22
  285.1 1.5 fusion.16
  286.6 66.0 %reduce-scatter.5.cloned.1.call-done = bf16[32,8192]{1,0:T(8,128)(2,1)} async-done(((bf16[256,8192]{1,0:T(8,128)(2,1)}), bf16[32,8192]{1,0:T(8,128)(2,1)}) %reduce-scatter.5.cloned.1.call-update) | async-done | bytes 524304 | tf_op jit(solution)/shard_map/reduce_scatter | solution.py:92
  352.6 4.7 %multiply_add_fusion = (f32[32,8192]{1,0:T(8,128)}, f32[32,8192]{1,0:T(8,128)}, f32[32,8192]{1,0:T(8,128)}, f32[32,8192]{1,0:T(8,128)}) fusion(f32[256,8192]{1,0:T(8,128)} %param.14, s32[]{:T(128)S(6)} %select_n.17, f32[256,8192]{1,0:T(8,128)} %param.13, bf16[32,8192]{1,0:T(8,128)(2,1)} %reduce-scatter.5.cloned.1.call-done, f32[32,8192]{1,0:T(8,128)S(1)} %copy-done.5, ...), kind=kLoop, calls=%fused_computation.25 | loop fusion | flops 4980736 | bytes 8912900 | tf_op jit(solution)/shard_map/add | solution.py:108
  (24 shorter events, 0.2 us)
Async XLA Ops:
  7.2 0.8 copy-start
  7.2 54.9 %copy-start.6 = (f32[8192]{0:T(1024)S(1)}, f32[8192]{0:T(1024)}, u32[]{:S(2)}) copy-start(f32[8192]{0:T(1024)} %param.17) | copy-start | bytes 98308
  7.2 38.9 %all-gather.3.cloned.1.call-start = ((), (), s32[]{:S(2)}) async-start(), calls=%async_computation.2 | async-start | bytes 1114112 | tf_op jit(solution)/shard_map/all_gather | solution.py:45
  11.2 273.0 %reduce-scatter.3.cloned.1.call-start = ((), (), s32[]{:S(2)}) async-start(), calls=%async_computation.3 | async-start | bytes 557056 | tf_op jit(solution)/shard_map/reduce_scatter | solution.py:74
  46.1 16.0 %copy-start.3 = (f32[256,8192]{1,0:T(8,128)S(1)}, f32[256,8192]{1,0:T(8,128)}, u32[]{:S(2)}) copy-start(f32[256,8192]{1,0:T(8,128)} %param.14) | copy-start | bytes 25165828
  46.1 16.0 %copy-start.4 = (bf16[2,1024,256]{2,1,0:T(8,128)(2,1)S(1)}, bf16[2,1024,256]{2,1,0:T(8,128)(2,1)}, u32[]{:S(2)}) copy-start(bf16[2,1024,256]{2,1,0:T(8,128)(2,1)} %all-gather.3.cloned.1.call-done) | copy-start | bytes 3145732
  105.0 20.2 %copy-start.2 = (f32[1024,8192]{1,0:T(8,128)S(1)}, f32[1024,8192]{1,0:T(8,128)}, u32[]{:S(2)}) copy-start(f32[1024,8192]{1,0:T(8,128)} %get-tuple-element.19) | copy-start | bytes 100663296
  159.7 197.6 %copy-start.1 = (bf16[1,128,256]{2,1,0:T(8,128)(2,1)S(1)}, bf16[1,128,256]{2,1,0:T(8,128)(2,1)}, u32[]{:S(2)}) copy-start(bf16[1,128,256]{2,1,0:T(8,128)(2,1)} %param.9) | copy-start | bytes 196612
  191.0 161.6 %copy-start.5 = (f32[32,8192]{1,0:T(8,128)S(1)}, f32[32,8192]{1,0:T(8,128)}, u32[]{:S(2)}) copy-start(f32[32,8192]{1,0:T(8,128)} %param.15) | copy-start | bytes 3145732
  204.6 148.0 %reduce-scatter.5.cloned.1.call-start = ((), (), s32[]{:S(2)}) async-start(), calls=%async_computation.4 | async-start | bytes 4718592 | tf_op jit(solution)/shard_map/reduce_scatter | solution.py:92
Sparse Core Ops, SparseCore 0:
  11.4 34.6 all-gather.2
  204.7 60.0 reduce-scatter.2
  268.7 83.8 reduce-scatter.4
where the time goes:
time: 365 us
  blocking collectives  136 us (37%)
  waiting for transfers between devices  84 us (23%)
  other arithmetic  62.7 us (17%)
  matrix products  55.2 us (15%)
  between operations  16.3 us (4%)
  local copies, waits for them, and re-layouts  10.1 us (3%)
    psum x1, blocking collectives, local(): loss_sum = lax.psum(partial_loss, ('dp', 'proto'))  66.2 us
    reduce_scatter x1, waiting for transfers between devices, local(): lax.psum_scatter(lax.dot_general(rows_student, grad_logit, (((0,), (0,)),...  66 us
    reduce_sum x1, other arithmetic, local(): jnp.sum(prob_t * (log_total[:, None] - student_logit), axis=1)  31.3 us
    pmax x1, blocking collectives, local(): lax.pmax((jnp.max(student_logit, axis=1), jnp.max(teacher_logit, axis=1))...  29.6 us
    psum x1, blocking collectives, local(): lax.psum((jnp.sum(exp_s, axis=1), jnp.sum(exp_t, axis=1)), 'proto')  27.8 us
    all_gather x1, waiting for transfers between devices, local(): lax.all_gather(stacked, 'proto', axis=1, tiled=True)  18 us
    dot_general x1, matrix products, local(): jnp.dot(rows_student, student_w, preferred_element_type=jnp.float32)  16 us
    reduce_sum x1, other arithmetic, local(): jnp.sum(exp_t, axis=1)  15.3 us
  transfers between devices with their start and end apart: 3, of which 2 were waited for; matrix products, arithmetic and copies ran while one was open for 5% of the time, Pallas kernels for 0%

commit v1 on v0

--- a/solution.py
+++ b/solution.py
@@ -42,7 +42,9 @@
     unit_teacher, inv_teacher = unit_rows(raw_teacher)
     stacked = jnp.stack([unit_student, unit_teacher]).astype(jnp.bfloat16)
     gathered, image_ids = (
-        lax.all_gather(stacked, "proto", axis=1, tiled=True),
+        jnp.concatenate(
+            lax.all_to_all(jnp.stack([stacked] * lax.axis_size("proto")), "proto", 0, 0), axis=1
+        ),
         lax.all_gather(patch_image[0][picked], "proto", axis=0, tiled=True),
     )
     rows_student = gathered[0]

time: 365 us -> 362 us (level)
  waiting for transfers between devices: 84 us -> 66.8 us
  other arithmetic: 62.7 us -> 68.8 us
  starting transfers between devices: 0.12 us -> 5.95 us
  blocking collectives: 136 us -> 140 us
    all_gather x1 -> x0, waiting for transfers between devices: 18 us -> none  [local(): lax.all_gather(stacked, 'proto', axis=1, tiled=True)]
    reduce_sum x1, other arithmetic: 6.66 us -> 14.1 us  [local(): jnp.sum(exp_s, axis=1)]
    all_to_all x0 -> x1, starting transfers between devices: none -> 5.87 us  [local(): lax.all_to_all(jnp.stack([stacked] * lax.axis_size('proto')), 'proto', 0, 0)]
    unnamed x1, blocking collectives: 12.9 us -> 18.1 us
    unnamed x17 -> x15, local copies, waits for them, and re-layouts: 6.44 us -> 1.66 us
  transfers between devices with their start and end apart: 3 -> 3, of which waited for: 2 -> 1; matrix products, arithmetic and copies ran while one was open for 5% -> 5% of each run, Pallas kernels for 0% -> 0%
where the time goes in v1:
time: 362 us; the launch traced here: 361 us
  blocking collectives  140 us (39%)
  other arithmetic  68.8 us (19%)
  waiting for transfers between devices  66.8 us (18%)
  matrix products  55.9 us (15%)
  between operations  16.7 us (5%)
  local copies, waits for them, and re-layouts  6.45 us (2%)
  starting transfers between devices  5.95 us (2%)
    reduce_scatter x1, waiting for transfers between devices, local(): lax.psum_scatter(lax.dot_general(rows_student, grad_logit, (((0,), (0,)),...  66.8 us
    psum x1, blocking collectives, local(): loss_sum = lax.psum(partial_loss, ('dp', 'proto'))  66.6 us
    reduce_sum x1, other arithmetic, local(): jnp.sum(prob_t * (log_total[:, None] - student_logit), axis=1)  31.3 us
    psum x1, blocking collectives, local(): lax.psum((jnp.sum(exp_s, axis=1), jnp.sum(exp_t, axis=1)), 'proto')  27.8 us
    pmax x1, blocking collectives, local(): lax.pmax((jnp.max(student_logit, axis=1), jnp.max(teacher_logit, axis=1))...  27.6 us
    unnamed x1, blocking collectives  18.1 us
    dot_general x1, matrix products, local(): jnp.dot(rows_student, student_w, preferred_element_type=jnp.float32)  16.7 us
    reduce_sum x1, other arithmetic, local(): jnp.sum(exp_t, axis=1)  14.7 us
  transfers between devices with their start and end apart: 3, of which 1 were waited for; matrix products, arithmetic and copies ran while one was open for 5% of the time, Pallas kernels for 0%

profile of v1, /device:TPU:0, one launch (start us, length us, event | category | flops | bytes accessed | tf_op | source)
XLA Modules:
  0.0 360.7 jit_solution(7419126667572867382)
XLA Ops:
  7.2 0.7 fusion.27
  7.9 0.1 copy-done
  8.0 0.7 gather_fusion
  8.7 0.1 fusion.20
  8.8 1.5 gather_fusion.2
  10.3 0.1 fusion.19
  10.5 0.1 fusion.18
  10.6 1.1 stack.5
  11.7 5.9 %all-to-all-start = ((bf16[16,2,64,256]{3,2,1,0:T(8,128)(2,1)}), bf16[16,2,64,256]{3,2,1,0:T(8,128)(2,1)S(1)}, u32[]{:S(2)}, u32[]{:S(2)}) async-start(bf16[16,2,64,256]{3,2,1,0:T(8,128)(2,1)} %stack.5), calls=%async_computation | async-start | bytes 2097152 | tf_op jit(solution)/shard_map/all_to_all | solution.py:46
  17.6 1.4 gather_fusion.1
  19.0 1.2 dynamic-slice
  21.0 0.2 dynamic-update-slice
  21.2 18.1 %all-reduce = s32[1024]{0:T(1024)S(1)} all-reduce(s32[1024]{0:T(1024)S(1)} %dynamic-update-slice), channel_id=2, replica_groups=mesh['dp'=8,'proto'=16] {'proto'}, use_global_device_ids=true, to_apply=%add | all-reduce | flops 1024 | bytes 8192
  39.3 0.1 convert_reduce_fusion
  39.4 0.1 fusion.25
  39.6 0.1 fusion.31
  39.7 16.7 %multiply_reduce_fusion.1 = (f32[1024]{0:T(1024)S(1)}, f32[1024,8192]{1,0:T(8,128)}) fusion(bf16[1024,256]{1,0:T(8,128)(2,1)S(1)} %bitcast.38, f32[256,8192]{1,0:T(8,128)} %param.13), kind=kOutput, calls=%fused_computation.10 | convolution fusion | flops 4313840640 | bytes 42471424 | tf_op jit(solution)/shard_map/dot_general | solution.py:55
  56.4 13.4 %fusion.1 = (f32[1024]{0:T(1024)S(1)}, f32[1024,8192]{1,0:T(8,128)}) fusion(f32[8192]{0:T(1024)S(1)} %copy-done.3, bf16[1024,256]{1,0:T(8,128)(2,1)S(1)} %bitcast.41, f32[256,8192]{1,0:T(8,128)S(1)} %bitcast.37), kind=kOutput, calls=%fused_computation.9 | convolution fusion | flops 4322229248 | bytes 42504192 | tf_op jit(solution)/shard_map/dot_general | solution.py:57
  69.9 27.6 %all-reduce.2 = (f32[1024]{0:T(1024)S(1)}, f32[1024]{0:T(1024)S(1)}) all-reduce(f32[1024]{0:T(1024)S(1)} %get-tuple-element.20, f32[1024]{0:T(1024)S(1)} %get-tuple-element.22), channel_id=1, replica_groups=mesh['dp'=8,'proto'=16] {'proto'}, use_global_device_ids=true, to_apply=%region_4.0 | all-reduce | flops 2048 | bytes 16384 | tf_op jit(solution)/shard_map/pmax | solution.py:59
  97.5 14.7 %fusion.3 = f32[1024]{0:T(1024)S(1)} fusion(f32[1024,8192]{1,0:T(8,128)} %get-tuple-element.23, f32[1024]{0:T(1024)S(1)} %get-tuple-element.9, f32[8192]{0:T(1024)S(1)} %copy-done.3), kind=kLoop, calls=%fused_computation.12 | loop fusion | flops 33553408 | bytes 33595392 | tf_op jit(solution)/shard_map/reduce_sum | solution.py:64
  112.2 14.1 %fusion = f32[1024]{0:T(1024)S(1)} fusion(f32[1024,8192]{1,0:T(8,128)} %get-tuple-element.21, f32[1024]{0:T(1024)S(1)} %get-tuple-element.8), kind=kLoop, calls=%fused_computation.8 | loop fusion | flops 25164800 | bytes 33562624 | tf_op jit(solution)/shard_map/reduce_sum | solution.py:64
  126.2 27.8 %all-reduce.1 = (f32[1024]{0:T(1024)S(1)}, f32[1024]{0:T(1024)S(1)}) all-reduce(f32[1024]{0:T(1024)S(1)} %fusion, f32[1024]{0:T(1024)S(1)} %fusion.3), channel_id=1, replica_groups=mesh['dp'=8,'proto'=16] {'proto'}, use_global_device_ids=true, to_apply=%region_6.0 | all-reduce | flops 2048 | bytes 16384 | tf_op jit(solution)/shard_map/psum | solution.py:64
  154.1 31.3 %multiply_reduce_fusion = (f32[1024]{0:T(1024)S(1)}, bf16[1024,8192]{1,0:T(8,128)(2,1)}) fusion(f32[1024,8192]{1,0:T(8,128)} %get-tuple-element.21, f32[1024]{0:T(1024)S(1)} %log_add_fusion, f32[1024]{0:T(1024)S(1)} %get-tuple-element.7, f32[1024]{0:T(1024)S(1)} %get-tuple-element.9, f32[1024,8192]{1,0:T(8,128)} %get-tuple-element.23, f32[8192]{0:T(1024)S(1)} %copy-done.3, ...), kind=kLoop, calls=%fused_computation.3 | loop fusion | flops 117439488 | bytes 83947520 | tf_op jit(solution)/shard_map/reduce_sum | solution.py:74
  185.4 13.6 %fusion.10 = bf16[1024,256]{1,0:T(8,128)(2,1)} fusion(bf16[1024,8192]{1,0:T(8,128)(2,1)} %get-tuple-element.15, f32[256,8192]{1,0:T(8,128)} %param.13), kind=kOutput, calls=%fused_computation.22 | convolution fusion | flops 4297326592 | bytes 25690112 | tf_op jit(solution)/shard_map/dot_general | solution.py:77
  199.0 0.0 reduce-scatter.5.cloned.1.call-start
  199.0 12.1 %convolution_convert_fusion = bf16[256,8192]{1,0:T(8,128)(2,1)} fusion(bf16[1024,256]{1,0:T(8,128)(2,1)S(1)} %bitcast.39, bf16[1024,8192]{1,0:T(8,128)(2,1)} %get-tuple-element.15), kind=kOutput, calls=%fused_computation.13 | convolution fusion | flops 4297064448 | bytes 21495808 | tf_op jit(solution)/shard_map/dot_general | solution.py:95
  211.1 0.6 multiply_reduce_fusion.2
  211.7 66.6 %psum.23 = f32[]{:T(128)} all-reduce(f32[]{:T(128)} %multiply_reduce_fusion.2), channel_id=1, replica_groups=mesh['dp'=8,'proto'=16] {'dp','proto'}, use_global_device_ids=true, to_apply=%region_16.0 | all-reduce | flops 1 | bytes 8 | tf_op jit(solution)/shard_map/psum | solution.py:102
  279.0 0.9 fusion.22
  279.9 1.5 fusion.16
  281.3 66.8 %reduce-scatter.5.cloned.1.call-done = bf16[32,8192]{1,0:T(8,128)(2,1)} async-done(((bf16[256,8192]{1,0:T(8,128)(2,1)}), bf16[32,8192]{1,0:T(8,128)(2,1)}) %reduce-scatter.5.cloned.1.call-update) | async-done | bytes 524304 | tf_op jit(solution)/shard_map/reduce_scatter | solution.py:94
  348.1 4.6 %multiply_add_fusion = (f32[32,8192]{1,0:T(8,128)}, f32[32,8192]{1,0:T(8,128)}, f32[32,8192]{1,0:T(8,128)}, f32[32,8192]{1,0:T(8,128)}) fusion(f32[256,8192]{1,0:T(8,128)} %param.14, s32[]{:T(128)S(6)} %select_n.17, f32[256,8192]{1,0:T(8,128)} %param.13, bf16[32,8192]{1,0:T(8,128)(2,1)} %reduce-scatter.5.cloned.1.call-done, f32[32,8192]{1,0:T(8,128)S(1)} %copy-done.2, ...), kind=kLoop, calls=%fused_computation.25 | loop fusion | flops 4980736 | bytes 8912900 | tf_op jit(solution)/shard_map/add | solution.py:110
  (24 shorter events, 0.2 us)
Async XLA Ops:
  7.2 0.8 copy-start
  7.2 49.2 %copy-start.3 = (f32[8192]{0:T(1024)S(1)}, f32[8192]{0:T(1024)}, u32[]{:S(2)}) copy-start(f32[8192]{0:T(1024)} %param.17) | copy-start | bytes 98308
  11.7 27.9 %all-to-all-start = ((bf16[16,2,64,256]{3,2,1,0:T(8,128)(2,1)}), bf16[16,2,64,256]{3,2,1,0:T(8,128)(2,1)S(1)}, u32[]{:S(2)}, u32[]{:S(2)}) async-start(bf16[16,2,64,256]{3,2,1,0:T(8,128)(2,1)} %stack.5), calls=%async_computation | async-start | bytes 2097152 | tf_op jit(solution)/shard_map/all_to_all | solution.py:46
  17.6 261.4 %reduce-scatter.3.cloned.1.call-start = ((), (), s32[]{:S(2)}) async-start(), calls=%async_computation.3 | async-start | bytes 557056 | tf_op jit(solution)/shard_map/reduce_scatter | solution.py:76
  39.6 16.8 %slice-start = ((s8[8388608]{0:T(1024)(128)(4,1)}), s8[4194304]{0:T(1024)(128)(4,1)S(1)}, s32[]{:S(2)}) async-start(s8[8388608]{0:T(1024)(128)(4,1)} %bitcast.36), calls=%async_computation.5 | async-start | bytes 8388608
  39.7 16.7 %slice-start.1 = ((s8[8388608]{0:T(1024)(128)(4,1)}), s8[4194304]{0:T(1024)(128)(4,1)S(1)}, s32[]{:S(2)}) async-start(s8[8388608]{0:T(1024)(128)(4,1)} %bitcast.36), calls=%async_computation.6 | async-start | bytes 8388608
  154.1 198.7 %copy-start.1 = (bf16[1,128,256]{2,1,0:T(8,128)(2,1)S(1)}, bf16[1,128,256]{2,1,0:T(8,128)(2,1)}, u32[]{:S(2)}) copy-start(bf16[1,128,256]{2,1,0:T(8,128)(2,1)} %param.9) | copy-start | bytes 196612
  185.4 162.8 %copy-start.2 = (f32[32,8192]{1,0:T(8,128)S(1)}, f32[32,8192]{1,0:T(8,128)}, u32[]{:S(2)}) copy-start(f32[32,8192]{1,0:T(8,128)} %param.15) | copy-start | bytes 3145732
  199.0 149.2 %reduce-scatter.5.cloned.1.call-start = ((), (), s32[]{:S(2)}) async-start(), calls=%async_computation.4 | async-start | bytes 4718592 | tf_op jit(solution)/shard_map/reduce_scatter | solution.py:94
Sparse Core Ops, SparseCore 0:
  199.1 61.0 reduce-scatter.2
  264.0 84.0 reduce-scatter.4
